TPU v7x, 32 devices: a whole 2x2x4 slice. The times are simulated.
32 devices in a mesh: dp: 4 (over x, core), ctx: 4 (over z), tp: 2 (over y).
Axes of the slice: x: 2, y: 2, z: 4, core: 2. Of those that a mesh axis runs over, the one named last changes fastest.
Arguments:
- tokens: bfloat16 [8192, 2048], P(('dp', 'ctx')), may hold values from -12 to 12, as said below
- gain_one: bfloat16 [2048], P(('dp', 'ctx')), may hold values from 0.099609375 to 1.8984375
- bias_one: bfloat16 [2048], P(('dp', 'ctx')), may hold values from -3 to 3
- w_query: bfloat16 [2048, 2048], P(('dp', 'ctx'), 'tp'), may hold values from -1 to 1, as said below
- w_keyval: bfloat16 [2048, 256], P(('dp', 'ctx')), may hold values from -0.125 to 0.125
- w_out: bfloat16 [2048, 2048], P(('dp', 'ctx'), 'tp'), may hold values from -2 to 2
- gain_two: bfloat16 [2048], P(('dp', 'ctx')), may hold values from 0.099609375 to 1.8984375
- bias_two: bfloat16 [2048], P(('dp', 'ctx')), may hold values from -3 to 3
- w_up: bfloat16 [2048, 8192], P(('dp', 'ctx'), 'tp'), may hold values from -1 to 1, as said below
- w_down: bfloat16 [2048, 8192], P(('dp', 'ctx'), 'tp'), may hold values from -0.0625 to 0.0625
- grad_out: bfloat16 [8192, 2048], P(('dp', 'ctx')), may hold values from -6 to 6
Outputs:
- layer_out: bfloat16 [8192, 2048], P(('dp', 'ctx'))
- input_grad: float32 [8192, 2048], P(('dp', 'ctx'))
- grad_gain_one: float32 [2048], P(('dp', 'ctx'))
- grad_bias_one: float32 [2048], P(('dp', 'ctx'))
- grad_query: float32 [2048, 2048], P(('dp', 'ctx'), 'tp')
- grad_keyval: float32 [2048, 256], P(('dp', 'ctx'))
- grad_out_proj: float32 [2048, 2048], P(('dp', 'ctx'), 'tp')
- grad_gain_two: float32 [2048], P(('dp', 'ctx'))
- grad_bias_two: float32 [2048], P(('dp', 'ctx'))
- grad_up: float32 [2048, 8192], P(('dp', 'ctx'), 'tp')
- grad_down: float32 [2048, 8192], P(('dp', 'ctx'), 'tp')
- rms_values: float32 [3], replicated
Inputs may be any that keep to these rules, and one draw needn't show every extreme that they name: `tokens`: real-valued activations. `w_query`: real-valued projection weights. `w_up`: real-valued projection weights.
All inputs are finite; a program needn't handle non-finite values.
Results may differ from a plain program's by a relative error of at most 0.015.
Values may be sent and summed in bfloat16 or wider, within the bound.
No kernel may reach another device: no remote copies, remote signals or barrier semaphores. Data moves between devices by JAX's collectives and lax.ppermute only.
A program may use at most 256 MiB of HBM per device.

v0:
```python
import jax
import jax.numpy as jnp
from jax import lax
from jax.sharding import PartitionSpec as P

BLOCK = 256
eps_norm = 1e-05
neg_large = -1e30


def layer_norm(values, gain, shift):
    center = values - jnp.mean(values, axis=-1, keepdims=True)
    spread = jnp.mean(center * center, axis=-1, keepdims=True)
    return center * lax.rsqrt(spread + eps_norm) * gain + shift


def gelu_tanh(values):
    return jax.nn.gelu(values, approximate=True)


def last_dot(left, right):
    return lax.dot_general(
        left, right, (((1,), (1,)), ((), ())), preferred_element_type=jnp.float32
    )


def first_dot(left, right):
    return lax.dot_general(
        left, right, (((0,), (0,)), ((), ())), preferred_element_type=jnp.float32
    )


def body(
    tokens, gain_one, bias_one, w_query, w_keyval, w_out, gain_two, bias_two, w_up, w_down, grad_out
):
    rows = tokens.shape[0]
    width = tokens.shape[1]
    head_size = w_keyval.shape[1] // 2
    local_heads = w_query.shape[1] // head_size
    scale = head_size ** (-0.5)
    ctx_index = lax.axis_index("ctx")
    tile_count = ctx_index + 1
    stream = tokens.astype(jnp.float32)
    full_gain_one, full_bias_one, query_full, keyval_full, out_full = (
        lax.all_gather(gain_one, ("dp", "ctx"), axis=0, tiled=True),
        lax.all_gather(bias_one, ("dp", "ctx"), axis=0, tiled=True),
        lax.all_gather(w_query, ("dp", "ctx"), axis=0, tiled=True),
        lax.all_gather(w_keyval, ("dp", "ctx"), axis=0, tiled=True),
        lax.all_gather(w_out, ("dp", "ctx"), axis=0, tiled=True),
    )
    normed_one, norm_one_pull = jax.vjp(
        layer_norm, stream, full_gain_one.astype(jnp.float32), full_bias_one.astype(jnp.float32)
    )
    normed_low = normed_one.astype(jnp.bfloat16)
    queries = jnp.dot(normed_low, query_full, preferred_element_type=jnp.float32).astype(
        jnp.bfloat16
    )
    keyvals = jnp.dot(normed_low, keyval_full, preferred_element_type=jnp.float32).astype(
        jnp.bfloat16
    )
    keyval_all = lax.all_gather(keyvals, "ctx", axis=0, tiled=True)
    keys_all = keyval_all[:, :head_size]
    values_all = keyval_all[:, head_size:]
    query_heads = queries.reshape(rows, local_heads, head_size)
    query_block = (ctx_index * rows + jnp.arange(rows, dtype=jnp.int32)) // BLOCK

    def tile_scores(tile):
        start = tile * rows
        key_tile = lax.dynamic_slice_in_dim(keys_all, start, rows, 0)
        value_tile = lax.dynamic_slice_in_dim(values_all, start, rows, 0)
        scores = (
            jnp.einsum("qhd,kd->hqk", query_heads, key_tile, preferred_element_type=jnp.float32)
            * scale
        )
        key_block = (start + jnp.arange(rows, dtype=jnp.int32)) // BLOCK
        allowed = (key_block[None, :] <= query_block[:, None])[None]
        return (scores, allowed, key_tile, value_tile)

    def max_step(tile, carry):
        run_max, run_sum = carry
        scores, allowed, key_tile, value_tile = tile_scores(tile)
        masked = jnp.where(allowed, scores, neg_large)
        new_max = jnp.maximum(run_max, jnp.max(masked, axis=-1))
        run_sum = run_sum * jnp.exp(run_max - new_max) + jnp.sum(
            jnp.exp(masked - new_max[..., None]), axis=-1
        )
        return (new_max, run_sum)

    start_max = jnp.full((local_heads, rows), neg_large, jnp.float32)
    start_sum = jnp.zeros((local_heads, rows), jnp.float32)
    row_max, row_sum = lax.fori_loop(0, tile_count, max_step, (start_max, start_sum))
    log_total = row_max + jnp.log(row_sum)

    def value_step(tile, accum):
        scores, allowed, key_tile, value_tile = tile_scores(tile)
        probs = jnp.where(allowed, jnp.exp(scores - log_total[..., None]), 0.0)
        return accum + jnp.einsum(
            "hqk,kd->qhd",
            probs.astype(jnp.bfloat16),
            value_tile,
            preferred_element_type=jnp.float32,
        )

    attn_accum = lax.fori_loop(
        0, tile_count, value_step, jnp.zeros((rows, local_heads, head_size), jnp.float32)
    )
    attn_low = attn_accum.reshape(rows, local_heads * head_size).astype(jnp.bfloat16)
    branch_attn = lax.psum(last_dot(attn_low, out_full).astype(jnp.bfloat16), "tp").astype(
        jnp.float32
    )
    hidden = stream + branch_attn
    full_gain_two, full_bias_two, up_full, down_full = (
        lax.all_gather(gain_two, ("dp", "ctx"), axis=0, tiled=True),
        lax.all_gather(bias_two, ("dp", "ctx"), axis=0, tiled=True),
        lax.all_gather(w_up, ("dp", "ctx"), axis=0, tiled=True),
        lax.all_gather(w_down, ("dp", "ctx"), axis=0, tiled=True),
    )
    normed_two, norm_two_pull = jax.vjp(
        layer_norm, hidden, full_gain_two.astype(jnp.float32), full_bias_two.astype(jnp.float32)
    )
    normed_two_low = normed_two.astype(jnp.bfloat16)
    pre_act = jnp.dot(normed_two_low, up_full, preferred_element_type=jnp.float32)
    act_value, gelu_pull = jax.vjp(gelu_tanh, pre_act)
    act_low = act_value.astype(jnp.bfloat16)
    branch_mlp = lax.psum(last_dot(act_low, down_full).astype(jnp.bfloat16), "tp").astype(
        jnp.float32
    )
    result = hidden + branch_mlp
    square_sums = lax.psum(
        jnp.stack(
            [
                jnp.sum(result * result),
                jnp.sum(branch_attn * branch_attn),
                jnp.sum(branch_mlp * branch_mlp),
            ]
        ),
        ("dp", "ctx"),
    )
    entry_count = rows * lax.axis_size("dp") * lax.axis_size("ctx") * width
    rms_values = jnp.sqrt(square_sums / entry_count)
    grad_result = grad_out.astype(jnp.float32)
    grad_act = jnp.dot(grad_out, down_full, preferred_element_type=jnp.float32)
    grad_down = first_dot(grad_out, act_low)
    grad_pre_low = gelu_pull(grad_act)[0].astype(jnp.bfloat16)
    grad_up = first_dot(normed_two_low, grad_pre_low)
    grad_normed_two = lax.psum(last_dot(grad_pre_low, up_full).astype(jnp.bfloat16), "tp").astype(
        jnp.float32
    )
    grad_hidden_norm, grad_gain_two, grad_bias_two = norm_two_pull(grad_normed_two)
    grad_hidden = grad_result + grad_hidden_norm
    grad_gain_two, grad_bias_two, grad_up, grad_down = (
        lax.psum_scatter(grad_gain_two, ("dp", "ctx"), scatter_dimension=0, tiled=True),
        lax.psum_scatter(grad_bias_two, ("dp", "ctx"), scatter_dimension=0, tiled=True),
        lax.psum_scatter(grad_up, ("dp", "ctx"), scatter_dimension=0, tiled=True),
        lax.psum_scatter(grad_down, ("dp", "ctx"), scatter_dimension=0, tiled=True),
    )
    grad_branch_low = grad_hidden.astype(jnp.bfloat16)
    grad_out_proj = first_dot(grad_branch_low, attn_low)
    grad_heads_low = jnp.dot(grad_branch_low, out_full, preferred_element_type=jnp.float32).astype(
        jnp.bfloat16
    )
    grad_heads = grad_heads_low.reshape(rows, local_heads, head_size)
    row_delta = jnp.sum(grad_heads.astype(jnp.float32) * attn_accum, axis=-1).T

    def back_step(tile, carry):
        grad_query_acc, grad_keyval_all = carry
        scores, allowed, key_tile, value_tile = tile_scores(tile)
        probs = jnp.where(allowed, jnp.exp(scores - log_total[..., None]), 0.0)
        grad_probs = jnp.einsum(
            "qhd,kd->hqk", grad_heads, value_tile, preferred_element_type=jnp.float32
        )
        grad_scores = (probs * (grad_probs - row_delta[..., None])).astype(jnp.bfloat16)
        grad_query_acc = grad_query_acc + jnp.einsum(
            "hqk,kd->qhd", grad_scores, key_tile, preferred_element_type=jnp.float32
        )
        grad_key_tile = (
            jnp.einsum("hqk,qhd->kd", grad_scores, query_heads, preferred_element_type=jnp.float32)
            * scale
        )
        grad_value_tile = jnp.einsum(
            "hqk,qhd->kd",
            probs.astype(jnp.bfloat16),
            grad_heads,
            preferred_element_type=jnp.float32,
        )
        grad_keyval_all = lax.dynamic_update_slice_in_dim(
            grad_keyval_all,
            jnp.concatenate([grad_key_tile, grad_value_tile], axis=1),
            tile * rows,
            0,
        )
        return (grad_query_acc, grad_keyval_all)

    start_query = jnp.zeros((rows, local_heads, head_size), jnp.float32)
    start_keyval = jnp.zeros(keyval_all.shape, jnp.float32)
    grad_query_acc, grad_keyval_all = lax.fori_loop(
        0, tile_count, back_step, (start_query, start_keyval)
    )
    grad_query_low = (
        (grad_query_acc * scale).reshape(rows, local_heads * head_size).astype(jnp.bfloat16)
    )
    grad_keyval_mine = lax.psum_scatter(
        grad_keyval_all.astype(jnp.bfloat16), "ctx", scatter_dimension=0, tiled=True
    )
    grad_normed_query = last_dot(grad_query_low, query_full)
    grad_normed_part, grad_keyval_sum = (
        lax.psum(grad_normed_query.astype(jnp.bfloat16), "tp").astype(jnp.float32),
        lax.psum(grad_keyval_mine, "tp").astype(jnp.float32),
    )
    grad_keyval_low = grad_keyval_sum.astype(jnp.bfloat16)
    grad_normed_one = grad_normed_part + last_dot(grad_keyval_low, keyval_full)
    grad_query = first_dot(normed_low, grad_query_low)
    grad_keyval = first_dot(normed_low, grad_keyval_low)
    grad_stream_norm, grad_gain_one, grad_bias_one = norm_one_pull(grad_normed_one)
    input_grad = grad_hidden + grad_stream_norm
    grad_gain_one, grad_bias_one, grad_query, grad_keyval, grad_out_proj = (
        lax.psum_scatter(grad_gain_one, ("dp", "ctx"), scatter_dimension=0, tiled=True),
        lax.psum_scatter(grad_bias_one, ("dp", "ctx"), scatter_dimension=0, tiled=True),
        lax.psum_scatter(grad_query, ("dp", "ctx"), scatter_dimension=0, tiled=True),
        lax.psum_scatter(grad_keyval, ("dp", "ctx"), scatter_dimension=0, tiled=True),
        lax.psum_scatter(grad_out_proj, ("dp", "ctx"), scatter_dimension=0, tiled=True),
    )
    return (
        result.astype(jnp.bfloat16),
        input_grad,
        grad_gain_one,
        grad_bias_one,
        grad_query,
        grad_keyval,
        grad_out_proj,
        grad_gain_two,
        grad_bias_two,
        grad_up,
        grad_down,
        rms_values,
    )


def solution(mesh):
    return jax.shard_map(
        body,
        mesh=mesh,
        in_specs=(
            P(("dp", "ctx"), None),
            P(("dp", "ctx")),
            P(("dp", "ctx")),
            P(("dp", "ctx"), "tp"),
            P(("dp", "ctx"), None),
            P(("dp", "ctx"), "tp"),
            P(("dp", "ctx")),
            P(("dp", "ctx")),
            P(("dp", "ctx"), "tp"),
            P(("dp", "ctx"), "tp"),
            P(("dp", "ctx"), None),
        ),
        out_specs=(
            P(("dp", "ctx"), None),
            P(("dp", "ctx"), None),
            P(("dp", "ctx")),
            P(("dp", "ctx")),
            P(("dp", "ctx"), "tp"),
            P(("dp", "ctx"), None),
            P(("dp", "ctx"), "tp"),
            P(("dp", "ctx")),
            P(("dp", "ctx")),
            P(("dp", "ctx"), "tp"),
            P(("dp", "ctx"), "tp"),
            P(),
        ),
        check_vma=False,
    )
```

profile of v0, /device:TPU:0, one launch (start us, length us, event | category | flops | bytes accessed | tf_op | source)
XLA Modules:
  0.0 1833.9 jit_solution(2962413026030763452)
XLA Ops:
  8.0 33.8 %all-gather.1 = bf16[16,1,128]{2,1,0:T(2,128)(2,1)S(1)} all-gather(bf16[1,1,128]{2,1,0:T(2,128)(2,1)} %bitcast.192), channel_id=1, replica_groups=mesh['dp'=4,'ctx'=4,'tp'=2] {'dp','ctx'}, dimensions={0}, use_global_device_ids=true | all-gather | bytes 4352 | tf_op jit(solution)/shard_map/all_gather | solution.py:46
  41.8 28.4 %all-gather = bf16[16,1,128]{2,1,0:T(2,128)(2,1)S(1)} all-gather(bf16[1,1,128]{2,1,0:T(2,128)(2,1)} %bitcast.193), channel_id=1, replica_groups=mesh['dp'=4,'ctx'=4,'tp'=2] {'dp','ctx'}, dimensions={0}, use_global_device_ids=true | all-gather | bytes 4352 | tf_op jit(solution)/shard_map/all_gather | solution.py:45
  82.6 25.4 %all-gather.13.cloned.1.call-done = bf16[2048,256]{1,0:T(8,128)(2,1)} async-done(((bf16[512,256]{1,0:T(8,128)(2,1)}), bf16[2048,256]{1,0:T(8,128)(2,1)}) %all-gather.13.cloned.1.call-update) | async-done | bytes 1048592 | tf_op jit(solution)/shard_map/all_gather | solution.py:61
  110.3 50.2 %all-gather.15.cloned.1.call-done = bf16[2048,1024]{1,0:T(8,128)(2,1)} async-done(((bf16[128,1024]{1,0:T(8,128)(2,1)}), bf16[2048,1024]{1,0:T(8,128)(2,1)}) %all-gather.15.cloned.1.call-update) | async-done | bytes 4194320 | tf_op jit(solution)/shard_map/all_gather | solution.py:47
  180.7 31.1 %all-gather.17.cloned.1.call-done = bf16[2048,1024]{1,0:T(8,128)(2,1)} async-done(((bf16[128,1024]{1,0:T(8,128)(2,1)}), bf16[2048,1024]{1,0:T(8,128)(2,1)}) %all-gather.17.cloned.1.call-update) | async-done | bytes 4194320 | tf_op jit(solution)/shard_map/all_gather | solution.py:49
  219.2 29.9 %all-gather.3 = bf16[16,1,128]{2,1,0:T(2,128)(2,1)S(1)} all-gather(bf16[1,1,128]{2,1,0:T(2,128)(2,1)S(1)} %bitcast.194), channel_id=1, replica_groups=mesh['dp'=4,'ctx'=4,'tp'=2] {'dp','ctx'}, dimensions={0}, use_global_device_ids=true | all-gather | bytes 4352 | tf_op jit(solution)/shard_map/all_gather | solution.py:114
  249.1 29.0 %all-gather.2 = bf16[16,1,128]{2,1,0:T(2,128)(2,1)S(1)} all-gather(bf16[1,1,128]{2,1,0:T(2,128)(2,1)S(1)} %bitcast.195), channel_id=1, replica_groups=mesh['dp'=4,'ctx'=4,'tp'=2] {'dp','ctx'}, dimensions={0}, use_global_device_ids=true | all-gather | bytes 4352 | tf_op jit(solution)/shard_map/all_gather | solution.py:113
  282.7 125.9 %all-gather.21.cloned.1.call-done = bf16[2048,4096]{1,0:T(8,128)(2,1)} async-done(((bf16[128,4096]{1,0:T(8,128)(2,1)}), bf16[2048,4096]{1,0:T(8,128)(2,1)}) %all-gather.21.cloned.1.call-update) | async-done | bytes 16777232 | tf_op jit(solution)/shard_map/all_gather | solution.py:116
  408.6 14.9 fusion.111
  423.5 112.6 %all-gather.19.cloned.1.call-done = bf16[2048,4096]{1,0:T(8,128)(2,1)} async-done(((bf16[128,4096]{1,0:T(8,128)(2,1)}), bf16[2048,4096]{1,0:T(8,128)(2,1)}) %all-gather.19.cloned.1.call-update) | async-done | bytes 16777232 | tf_op jit(solution)/shard_map/all_gather | solution.py:115
  536.1 21.0 %fusion.81 = (bf16[512,4096]{1,0:T(8,128)(2,1)S(1)}, f32[512,4096]{1,0:T(8,128)}) fusion(f32[512,4096]{1,0:T(8,128)} %fusion.111, bf16[2048,4096]{1,0:T(8,128)(2,1)} %all-gather.19.cloned.1.call-done, bf16[512,2048]{1,0:T(8,128)(2,1)} %all-reduce.11.cloned.1.call-done, bf16[512,2048]{1,0:T(8,128)(2,1)S(1)} %copy-done, f32[2048]{0:T(1024)S(1)} %bitcast.190, ...), kind=kOutput, calls=%fused_computation.119 | convolution fusion | flops 8640266240 | bytes 41963520 | tf_op jit(solution)/shard_map/dot_general | solution.py:122
  557.1 18.5 %convolution_convert_fusion.3 = bf16[512,2048]{1,0:T(8,128)(2,1)} fusion(bf16[2048,4096]{1,0:T(8,128)(2,1)} %all-gather.21.cloned.1.call-done, f32[512,4096]{1,0:T(8,128)} %get-tuple-element.583), kind=kOutput, calls=%fused_computation.160 | convolution fusion | flops 8609857536 | bytes 27262976 | tf_op jit(solution)/shard_map/dot_general | solution.py:22
  575.6 13.4 convolution_convert_fusion.2
  591.0 104.7 %all-reduce.15.cloned.1.call-done = (bf16[512,2048]{1,0:T(8,128)(2,1)}, bf16[512,2048]{1,0:T(8,128)(2,1)}) async-done(((bf16[512,2048]{1,0:T(8,128)(2,1)}, bf16[512,2048]{1,0:T(8,128)(2,1)}), (bf16[512,2048]{1,0:T(8,128)(2,1)}, bf16[512,2048]{1,0:T(8,128)(2,1)})) %all-reduce.15.cloned.1.call-update) | async-done | bytes 4194320 | tf_op jit(solution)/shard_map/psum | solution.py:125
  740.2 56.9 %reduce-scatter.7.cloned.1.call-done = bf16[512,256]{0,1:T(8,128)(2,1)} async-done(((bf16[2048,256]{0,1:T(8,128)(2,1)}), bf16[512,256]{0,1:T(8,128)(2,1)}) %reduce-scatter.7.cloned.1.call-update) | async-done | bytes 262160 | tf_op jit(solution)/shard_map/reduce_scatter | solution.py:202
  797.2 21.1 %convolution_bitcast_fusion.1 = f32[2048,4096]{0,1:T(8,128)} fusion(bf16[512,2048]{1,0:T(8,128)(2,1)} %param.27, f32[512,4096]{1,0:T(8,128)} %get-tuple-element.583), kind=kOutput, calls=%fused_computation.110 | convolution fusion | flops 8608808960 | bytes 44040192 | tf_op jit(solution)/shard_map/dot_general | solution.py:28
  818.4 49.2 %all-reduce.13.cloned.1.call-done = (bf16[512,2048]{1,0:T(8,128)(2,1)}, bf16[512,256]{0,1:T(8,128)(2,1)}) async-done(((bf16[512,2048]{1,0:T(8,128)(2,1)}, bf16[512,256]{0,1:T(8,128)(2,1)}), (bf16[512,2048]{1,0:T(8,128)(2,1)}, bf16[512,256]{0,1:T(8,128)(2,1)})) %all-reduce.13.cloned.1.call-update) | async-done | bytes 2359312 | tf_op jit(solution)/shard_map/psum | solution.py:207
  890.0 25.4 %fusion.106 = f32[2048,4096]{1,0:T(8,128)} fusion(bf16[512,4096]{1,0:T(8,128)(2,1)} %copy-done.33, bf16[512,2048]{1,0:T(8,128)(2,1)} %all-reduce.11.cloned.1.call-done, bf16[512,2048]{1,0:T(8,128)(2,1)S(1)} %copy-done, f32[2048]{0:T(1024)S(1)} %bitcast.191, f32[2048]{0:T(1024)S(1)} %bitcast.187, f32[512]{0:T(512)S(1)} %fusion.104, ...), kind=kOutput, calls=%fused_computation.183 | convolution fusion | flops 8598323200 | bytes 41963520 | tf_op jit(solution)/shard_map/dot_general | solution.py:28
  926.7 66.4 %all-reduce.4 = (f32[2048]{0:T(1024)S(1)}, f32[2048]{0:T(1024)S(1)}, f32[2048]{0:T(1024)S(1)}, f32[2048]{0:T(1024)S(1)}, f32[3]{0:T(128)S(1)}) all-reduce(f32[2048]{0:T(1024)S(1)} %get-tuple-element.498, f32[2048]{0:T(1024)S(1)} %get-tuple-element.503, ...), channel_id=3, replica_groups=mesh['dp'=4,'ctx'=4,'tp'=2] {'dp','ctx'}, use_global_device_ids=true, to_apply=%region_24.25.clone | all-reduce | flops 8195 | bytes 65560
  1002.7 203.6 %reduce-scatter.17.cloned.1.call-done = f32[128,4096]{0,1:T(8,128)} async-done(((f32[2048,4096]{0,1:T(8,128)}), f32[128,4096]{0,1:T(8,128)}) %reduce-scatter.17.cloned.1.call-update) | async-done | bytes 2097168 | tf_op jit(solution)/shard_map/reduce_scatter | solution.py:155
  1209.1 61.9 %reduce-scatter.11.cloned.1.call-done = f32[128,256]{1,0:T(8,128)} async-done(((f32[2048,256]{1,0:T(8,128)}), f32[128,256]{1,0:T(8,128)}) %reduce-scatter.11.cloned.1.call-update) | async-done | bytes 131088 | tf_op jit(solution)/shard_map/reduce_scatter | solution.py:220
  1271.0 108.8 %reduce-scatter.9.cloned.1.call-done = f32[128,1024]{1,0:T(8,128)} async-done(((f32[2048,1024]{1,0:T(8,128)}), f32[128,1024]{1,0:T(8,128)}) %reduce-scatter.9.cloned.1.call-update) | async-done | bytes 524304 | tf_op jit(solution)/shard_map/reduce_scatter | solution.py:219
  1379.8 109.4 %reduce-scatter.13.cloned.1.call-done = f32[128,1024]{1,0:T(8,128)} async-done(((f32[2048,1024]{1,0:T(8,128)}), f32[128,1024]{1,0:T(8,128)}) %reduce-scatter.13.cloned.1.call-update) | async-done | bytes 524304 | tf_op jit(solution)/shard_map/reduce_scatter | solution.py:221
  1489.3 337.7 %reduce-scatter.15.cloned.1.call-done = f32[128,4096]{1,0:T(8,128)} async-done(((f32[2048,4096]{1,0:T(8,128)}), f32[128,4096]{1,0:T(8,128)}) %reduce-scatter.15.cloned.1.call-update) | async-done | bytes 2097168 | tf_op jit(solution)/shard_map/reduce_scatter | solution.py:154
  (174 shorter events, 161.7 us)
Async XLA Ops:
  7.2 68.4 %copy-start = (bf16[512,2048]{1,0:T(8,128)(2,1)S(1)}, bf16[512,2048]{1,0:T(8,128)(2,1)}, u32[]{:S(2)}) copy-start(bf16[512,2048]{1,0:T(8,128)(2,1)} %param.17) | copy-start | bytes 6291460
  7.2 70.6 %all-gather.11.cloned.1.call-start = ((), (), s32[]{:S(2)}) async-start(), calls=%async_computation.6 | async-start | bytes 1114112 | tf_op jit(solution)/shard_map/all_gather | solution.py:48
  7.9 100.2 %all-gather.13.cloned.1.call-start = ((), (), s32[]{:S(2)}) async-start(), calls=%async_computation.7 | async-start | bytes 1310720 | tf_op jit(solution)/shard_map/all_gather | solution.py:61
  81.1 79.5 %all-gather.15.cloned.1.call-start = ((), (), s32[]{:S(2)}) async-start(), calls=%async_computation.8 | async-start | bytes 4456448 | tf_op jit(solution)/shard_map/all_gather | solution.py:47
  81.8 130.1 %all-gather.17.cloned.1.call-start = ((), (), s32[]{:S(2)}) async-start(), calls=%async_computation.9 | async-start | bytes 4456448 | tf_op jit(solution)/shard_map/all_gather | solution.py:49
  82.4 197.0 %all-reduce.11.cloned.1.call-start = ((), (), s32[]{:S(2)}) async-start(), calls=%async_computation.10 | async-start | bytes 4194304 | tf_op jit(solution)/shard_map/psum | solution.py:108
  180.7 37.0 %copy-start.13 = (bf16[512,8,128]{0,2,1:T(8,128)(2,1)}, bf16[512,8,128]{0,2,1:T(8,128)(2,1)S(1)}, u32[]{:S(2)}) copy-start(bf16[512,8,128]{0,2,1:T(8,128)(2,1)S(1)} %convert_element_type.113) | copy-start | bytes 3145732
  217.8 31.4 %copy-start.30 = (bf16[128]{0:T(256)(128)(2,1)S(1)}, bf16[128]{0:T(256)(128)(2,1)}, u32[]{:S(2)}) copy-start(bf16[128]{0:T(256)(128)(2,1)} %param.23) | copy-start | bytes 772
  217.8 190.8 %all-gather.21.cloned.1.call-start = ((), (), s32[]{:S(2)}) async-start(), calls=%async_computation.12 | async-start | bytes 17825792 | tf_op jit(solution)/shard_map/all_gather | solution.py:116
  218.4 317.8 %all-gather.19.cloned.1.call-start = ((), (), s32[]{:S(2)}) async-start(), calls=%async_computation.11 | async-start | bytes 17825792 | tf_op jit(solution)/shard_map/all_gather | solution.py:115
  219.1 476.5 %all-reduce.15.cloned.1.call-start = ((), (), s32[]{:S(2)}) async-start(), calls=%async_computation.20 | async-start | bytes 8388608 | tf_op jit(solution)/shard_map/psum | solution.py:125
  249.1 287.0 %copy-start.27 = (f32[16,1,128]{2,1,0:T(1,128)}, f32[16,1,128]{2,1,0:T(1,128)S(1)}, u32[]{:S(2)}) copy-start(f32[16,1,128]{2,1,0:T(1,128)S(1)} %convert_element_type.139) | copy-start | bytes 24580
  557.1 18.5 %copy-start.33 = (bf16[512,4096]{1,0:T(8,128)(2,1)}, bf16[512,4096]{1,0:T(8,128)(2,1)S(1)}, u32[]{:S(2)}) copy-start(bf16[512,4096]{1,0:T(8,128)(2,1)S(1)} %get-tuple-element.582) | copy-start | bytes 12582916
  589.1 208.1 %reduce-scatter.7.cloned.1.call-start = ((), (), s32[]{:S(2)}) async-start(), calls=%async_computation.13 | async-start | bytes 1310720 | tf_op jit(solution)/shard_map/reduce_scatter | solution.py:202
  695.6 7.0 copy-start.6
  695.6 7.0 copy-start.8
  732.4 135.2 %all-reduce.13.cloned.1.call-start = ((), (), s32[]{:S(2)}) async-start(), calls=%async_computation.19 | async-start | bytes 4718592 | tf_op jit(solution)/shard_map/psum | solution.py:207
  797.2 409.1 %reduce-scatter.17.cloned.1.call-start = ((), (), s32[]{:S(2)}) async-start(), calls=%async_computation.18 | async-start | bytes 35651584 | tf_op jit(solution)/shard_map/reduce_scatter | solution.py:155
  818.3 452.7 %reduce-scatter.11.cloned.1.call-start = ((), (), s32[]{:S(2)}) async-start(), calls=%async_computation.15 | async-start | bytes 2228224 | tf_op jit(solution)/shard_map/reduce_scatter | solution.py:220
  871.3 508.6 %reduce-scatter.9.cloned.1.call-start = ((), (), s32[]{:S(2)}) async-start(), calls=%async_computation.14 | async-start | bytes 8912896 | tf_op jit(solution)/shard_map/reduce_scatter | solution.py:219
  878.9 610.3 %reduce-scatter.13.cloned.1.call-start = ((), (), s32[]{:S(2)}) async-start(), calls=%async_computation.16 | async-start | bytes 8912896 | tf_op jit(solution)/shard_map/reduce_scatter | solution.py:221
  889.3 937.6 %reduce-scatter.15.cloned.1.call-start = ((), (), s32[]{:S(2)}) async-start(), calls=%async_computation.17 | async-start | bytes 35651584 | tf_op jit(solution)/shard_map/reduce_scatter | solution.py:154
  919.4 5.3 copy-start.20
  922.7 73.3 %copy-start.24 = (f32[512]{0:T(512)S(1)}, f32[512]{0:T(512)}, u32[]{:S(2)}) copy-start(f32[512]{0:T(512)} %copy-done.23) | copy-start | bytes 6148
  (25 other events, 64.9 us)
Sparse Core Ops, SparseCore 0:
  10.2 40.6 all-gather.10
  81.2 26.8 all-gather.12
  110.3 50.1 all-gather.14
  162.6 49.2 all-gather.16
  217.9 61.4 all-reduce.10
  281.7 126.8 all-gather.20
  411.1 125.0 all-gather.18
  589.2 106.3 all-reduce.14
  732.5 64.5 reduce-scatter.6
  800.1 67.4 all-reduce.12
  871.8 334.3 reduce-scatter.16
  1210.4 60.5 reduce-scatter.10
  1276.2 103.5 reduce-scatter.8
  1384.9 104.3 reduce-scatter.12
  1494.5 332.3 reduce-scatter.14
where the time goes:
time: 1840 us; the launch traced here: 1830 us
  waiting for transfers between devices  1380 us (75%)
  blocking collectives  188 us (10%)
  matrix products  181 us (10%)
  other arithmetic  39.6 us (2%)
  local copies, waits for them, and re-layouts  27.3 us (1%)
    reduce_scatter x1, waiting for transfers between devices, body(): lax.psum_scatter(grad_up, ('dp', 'ctx'), scatter_dimension=0, tiled=True)  338 us
    reduce_scatter x1, waiting for transfers between devices, body(): lax.psum_scatter(grad_down, ('dp', 'ctx'), scatter_dimension=0, tiled=True)  204 us
    all_gather x1, waiting for transfers between devices, body(): lax.all_gather(w_down, ('dp', 'ctx'), axis=0, tiled=True)  126 us
    all_gather x1, waiting for transfers between devices, body(): lax.all_gather(w_up, ('dp', 'ctx'), axis=0, tiled=True)  113 us
    reduce_scatter x1, waiting for transfers between devices, body(): lax.psum_scatter(grad_out_proj, ('dp', 'ctx'), scatter_dimension=0, tiled...  109 us
    reduce_scatter x1, waiting for transfers between devices, body(): lax.psum_scatter(grad_query, ('dp', 'ctx'), scatter_dimension=0, tiled=True)  109 us
    psum x1, waiting for transfers between devices, body(): lax.psum(last_dot(act_low, down_full).astype(jnp.bfloat16), 'tp')  105 us
    dot_general x5, matrix products, first_dot(): lax.dot_general(left, right, (((0,), (0,)), ((), ())), preferred_element_...  66.7 us
  transfers between devices with their start and end apart: 15, of which 14 were waited for; matrix products, arithmetic and copies ran while one was open for 8% of the time, Pallas kernels for 0%

commit v1 on v0

--- a/solution.py
+++ b/solution.py
@@ -1,3 +1,4 @@
+import functools
 import jax
 import jax.numpy as jnp
 from jax import lax
@@ -6,6 +7,29 @@
 BLOCK = 256
 eps_norm = 1e-05
 neg_large = -1e30
+
+
+def map_object(load, link_axis):
+    x_next, v1, out_arr = (lax.axis_size(link_axis), lax.axis_index(link_axis), load.shape[0])
+    panels = [i0 * x_next if ii == 0 else i0 for ii, i0 in enumerate(load.shape)]
+    z1 = prior = load
+    r_now = lax.dynamic_update_slice_in_dim(
+        jnp.zeros(panels, load.dtype), load, v1 * out_arr, axis=0
+    )
+    for w in tuple(range(1, x_next // 2 + 1)):
+        z1 = lax.ppermute(z1, link_axis, [(ii, (ii + 1) % x_next) for ii in range(x_next)])
+        r_now = lax.dynamic_update_slice_in_dim(r_now, z1, (v1 - w) % x_next * out_arr, axis=0)
+        if 2 * w < x_next:
+            prior = lax.ppermute(
+                prior, link_axis, [(ii, (ii - 1) % x_next) for ii in range(x_next)]
+            )
+            r_now = lax.dynamic_update_slice_in_dim(
+                r_now, prior, (v1 + w) % x_next * out_arr, axis=0
+            )
+    return r_now
+
+
+point_stocks = functools.partial(map_object, link_axis=("dp", "ctx"))
 
 
 def layer_norm(values, gain, shift):
@@ -112,7 +136,7 @@
     full_gain_two, full_bias_two, up_full, down_full = (
         lax.all_gather(gain_two, ("dp", "ctx"), axis=0, tiled=True),
         lax.all_gather(bias_two, ("dp", "ctx"), axis=0, tiled=True),
-        lax.all_gather(w_up, ("dp", "ctx"), axis=0, tiled=True),
+        point_stocks(w_up),
         lax.all_gather(w_down, ("dp", "ctx"), axis=0, tiled=True),
     )
     normed_two, norm_two_pull = jax.vjp(

time: 1840 us -> 2020 us (1.098)
  blocking collectives: 188 us -> 264 us
  waiting for transfers between devices: 1380 us -> 1430 us
  local copies, waits for them, and re-layouts: 27.3 us -> 58.7 us
  starting transfers between devices: 1.06 us -> 30.1 us
    ppermute x0 -> x15, waiting for transfers between devices: none -> 285 us  [the longest x7 164 us: map_object(): lax.ppermute(prior, link_axis, [(ii, (ii - 1) % x_next) for ii in range(x...]
    all_gather x1, waiting for transfers between devices: 126 us -> 0.02 us  [body(): lax.all_gather(w_down, ('dp', 'ctx'), axis=0, tiled=True)]
    all_gather x1 -> x0, waiting for transfers between devices: 113 us -> none  [body(): lax.all_gather(w_up, ('dp', 'ctx'), axis=0, tiled=True)]
    all_gather x1, blocking collectives: 29.9 us -> 107 us  [body(): lax.all_gather(bias_two, ('dp', 'ctx'), axis=0, tiled=True)]
    ppermute x0 -> x15, starting transfers between devices: none -> 29.3 us  [the longest x7 19 us: map_object(): lax.ppermute(prior, link_axis, [(ii, (ii - 1) % x_next) for ii in range(x...]
    dynamic_update_slice x0 -> x16, local copies, waits for them, and re-layouts: none -> 24.5 us  [the longest x8 13.5 us: map_object(): lax.dynamic_update_slice_in_dim(r_now, z1, (v1 - w) % x_next * out_arr, a...]
  transfers between devices with their start and end apart: 15 -> 29, of which waited for: 14 -> 24; matrix products, arithmetic and copies ran while one was open for 8% -> 8% of each run, Pallas kernels for 0% -> 0%
where the time goes in v1:
time: 2020 us
  waiting for transfers between devices  1430 us (71%)
  blocking collectives  264 us (13%)
  matrix products  181 us (9%)
  local copies, waits for them, and re-layouts  58.7 us (3%)
  other arithmetic  39.6 us (2%)
  starting transfers between devices  30.1 us (1%)
    reduce_scatter x1, waiting for transfers between devices, body(): lax.psum_scatter(grad_up, ('dp', 'ctx'), scatter_dimension=0, tiled=True)  338 us
    reduce_scatter x1, waiting for transfers between devices, body(): lax.psum_scatter(grad_down, ('dp', 'ctx'), scatter_dimension=0, tiled=True)  204 us
    ppermute x7, waiting for transfers between devices, map_object(): lax.ppermute(prior, link_axis, [(ii, (ii - 1) % x_next) for ii in range(x...  164 us
    ppermute x8, waiting for transfers between devices, map_object(): lax.ppermute(z1, link_axis, [(ii, (ii + 1) % x_next) for ii in range(x_ne...  121 us
    reduce_scatter x1, waiting for transfers between devices, body(): lax.psum_scatter(grad_out_proj, ('dp', 'ctx'), scatter_dimension=0, tiled...  110 us
    reduce_scatter x1, waiting for transfers between devices, body(): lax.psum_scatter(grad_query, ('dp', 'ctx'), scatter_dimension=0, tiled=True)  109 us
    psum x1, waiting for transfers between devices, body(): lax.psum(last_dot(act_low, down_full).astype(jnp.bfloat16), 'tp')  107 us
    all_gather x1, blocking collectives, body(): lax.all_gather(bias_two, ('dp', 'ctx'), axis=0, tiled=True)  107 us
  transfers between devices with their start and end apart: 29, of which 24 were waited for; matrix products, arithmetic and copies ran while one was open for 8% of the time, Pallas kernels for 0%

profile of v1, /device:TPU:0, one launch (start us, length us, event | category | flops | bytes accessed | tf_op | source)
XLA Modules:
  0.0 2018.0 jit_solution(17091627043761234696)
XLA Ops:
  8.0 33.8 %all-gather.1 = bf16[16,1,128]{2,1,0:T(2,128)(2,1)S(1)} all-gather(bf16[1,1,128]{2,1,0:T(2,128)(2,1)} %bitcast.192), channel_id=1, replica_groups=mesh['dp'=4,'ctx'=4,'tp'=2] {'dp','ctx'}, dimensions={0}, use_global_device_ids=true | all-gather | bytes 4352 | tf_op jit(solution)/shard_map/all_gather | solution.py:70
  41.8 28.4 %all-gather = bf16[16,1,128]{2,1,0:T(2,128)(2,1)S(1)} all-gather(bf16[1,1,128]{2,1,0:T(2,128)(2,1)} %bitcast.193), channel_id=1, replica_groups=mesh['dp'=4,'ctx'=4,'tp'=2] {'dp','ctx'}, dimensions={0}, use_global_device_ids=true | all-gather | bytes 4352 | tf_op jit(solution)/shard_map/all_gather | solution.py:69
  82.7 25.4 %all-gather.12.cloned.1.call-done = bf16[2048,256]{1,0:T(8,128)(2,1)} async-done(((bf16[512,256]{1,0:T(8,128)(2,1)}), bf16[2048,256]{1,0:T(8,128)(2,1)}) %all-gather.12.cloned.1.call-update) | async-done | bytes 1048592 | tf_op jit(solution)/shard_map/all_gather | solution.py:85
  110.4 50.2 %all-gather.14.cloned.1.call-done = bf16[2048,1024]{1,0:T(8,128)(2,1)} async-done(((bf16[128,1024]{1,0:T(8,128)(2,1)}), bf16[2048,1024]{1,0:T(8,128)(2,1)}) %all-gather.14.cloned.1.call-update) | async-done | bytes 4194320 | tf_op jit(solution)/shard_map/all_gather | solution.py:71
  181.4 30.3 %all-gather.16.cloned.1.call-done = bf16[2048,1024]{1,0:T(8,128)(2,1)} async-done(((bf16[128,1024]{1,0:T(8,128)(2,1)}), bf16[2048,1024]{1,0:T(8,128)(2,1)}) %all-gather.16.cloned.1.call-update) | async-done | bytes 4194320 | tf_op jit(solution)/shard_map/all_gather | solution.py:73
  222.8 23.9 %collective-permute-done = bf16[128,4096]{1,0:T(8,128)(2,1)S(1)} collective-permute-done((bf16[128,4096]{1,0:T(8,128)(2,1)}, bf16[128,4096]{1,0:T(8,128)(2,1)S(1)}, u32[]{:S(2)}, u32[]{:S(2)}) %collective-permute-start) | collective-permute-done | bytes 1048608 | tf_op jit(solution)/shard_map/ppermute | solution.py:20
  246.7 20.8 %collective-permute-done.1 = bf16[128,4096]{1,0:T(8,128)(2,1)S(1)} collective-permute-done((bf16[128,4096]{1,0:T(8,128)(2,1)}, bf16[128,4096]{1,0:T(8,128)(2,1)S(1)}, u32[]{:S(2)}, u32[]{:S(2)}) %collective-permute-start.1) | collective-permute-done | bytes 1048608 | tf_op jit(solution)/shard_map/ppermute | solution.py:23
  270.6 21.2 %collective-permute-done.2 = bf16[128,4096]{1,0:T(8,128)(2,1)} collective-permute-done((bf16[128,4096]{1,0:T(8,128)(2,1)S(1)}, bf16[128,4096]{1,0:T(8,128)(2,1)}, u32[]{:S(2)}, u32[]{:S(2)}) %collective-permute-start.2) | collective-permute-done | bytes 1048608 | tf_op jit(solution)/shard_map/ppermute | solution.py:20
  291.8 72.1 %collective-permute-done.3 = bf16[128,4096]{1,0:T(8,128)(2,1)} collective-permute-done((bf16[128,4096]{1,0:T(8,128)(2,1)S(1)}, bf16[128,4096]{1,0:T(8,128)(2,1)}, u32[]{:S(2)}, u32[]{:S(2)}) %collective-permute-start.3) | collective-permute-done | bytes 1048608 | tf_op jit(solution)/shard_map/ppermute | solution.py:23
  377.5 107.3 %all-gather.3 = bf16[16,1,128]{2,1,0:T(2,128)(2,1)S(1)} all-gather(bf16[1,1,128]{2,1,0:T(2,128)(2,1)S(1)} %bitcast.194), channel_id=1, replica_groups=mesh['dp'=4,'ctx'=4,'tp'=2] {'dp','ctx'}, dimensions={0}, use_global_device_ids=true | all-gather | bytes 4352 | tf_op jit(solution)/shard_map/all_gather | solution.py:138
  484.8 28.3 %all-gather.2 = bf16[16,1,128]{2,1,0:T(2,128)(2,1)S(1)} all-gather(bf16[1,1,128]{2,1,0:T(2,128)(2,1)S(1)} %bitcast.195), channel_id=1, replica_groups=mesh['dp'=4,'ctx'=4,'tp'=2] {'dp','ctx'}, dimensions={0}, use_global_device_ids=true | all-gather | bytes 4352 | tf_op jit(solution)/shard_map/all_gather | solution.py:137
  677.3 20.1 collective-permute-done.14
  717.0 20.5 %fusion.81 = (bf16[512,4096]{1,0:T(8,128)(2,1)S(1)}, f32[512,4096]{1,0:T(8,128)}) fusion(f32[512,4096]{1,0:T(8,128)} %fusion.111, bf16[2048,4096]{1,0:T(8,128)(2,1)} %constant_dynamic-update-slice_fusion, bf16[512,2048]{1,0:T(8,128)(2,1)S(1)} %copy-done.6, bf16[512,2048]{1,0:T(8,128)(2,1)S(1)} %copy-done, f32[2048]{0:T(1024)S(1)} %bitcast.190, ...), kind=kOutput, calls=%fused_computation.119 | convolution fusion | flops 8640266240 | bytes 41963520 | tf_op jit(solution)/shard_map/dot_general | solution.py:146
  771.4 107.4 %all-reduce.15.cloned.1.call-done = (bf16[512,2048]{1,0:T(8,128)(2,1)}, bf16[512,2048]{1,0:T(8,128)(2,1)}) async-done(((bf16[512,2048]{1,0:T(8,128)(2,1)}, bf16[512,2048]{1,0:T(8,128)(2,1)}), (bf16[512,2048]{1,0:T(8,128)(2,1)}, bf16[512,2048]{1,0:T(8,128)(2,1)})) %all-reduce.15.cloned.1.call-update) | async-done | bytes 4194320 | tf_op jit(solution)/shard_map/psum | solution.py:149
  923.3 56.9 %reduce-scatter.7.cloned.1.call-done = bf16[512,256]{0,1:T(8,128)(2,1)} async-done(((bf16[2048,256]{0,1:T(8,128)(2,1)}), bf16[512,256]{0,1:T(8,128)(2,1)}) %reduce-scatter.7.cloned.1.call-update) | async-done | bytes 262160 | tf_op jit(solution)/shard_map/reduce_scatter | solution.py:226
  980.3 21.4 %convolution_bitcast_fusion.1 = f32[2048,4096]{0,1:T(8,128)} fusion(bf16[512,2048]{1,0:T(8,128)(2,1)} %param.27, f32[512,4096]{1,0:T(8,128)} %get-tuple-element.583), kind=kOutput, calls=%fused_computation.110 | convolution fusion | flops 8608808960 | bytes 44040192 | tf_op jit(solution)/shard_map/dot_general | solution.py:52
  1001.8 49.0 %all-reduce.13.cloned.1.call-done = (bf16[512,2048]{1,0:T(8,128)(2,1)}, bf16[512,256]{0,1:T(8,128)(2,1)}) async-done(((bf16[512,2048]{1,0:T(8,128)(2,1)}, bf16[512,256]{0,1:T(8,128)(2,1)}), (bf16[512,2048]{1,0:T(8,128)(2,1)}, bf16[512,256]{0,1:T(8,128)(2,1)})) %all-reduce.13.cloned.1.call-update) | async-done | bytes 2359312 | tf_op jit(solution)/shard_map/psum | solution.py:231
  1073.3 25.8 %fusion.106 = f32[2048,4096]{1,0:T(8,128)} fusion(bf16[512,4096]{1,0:T(8,128)(2,1)} %copy-done.39, bf16[512,2048]{1,0:T(8,128)(2,1)} %all-reduce.11.cloned.1.call-done, bf16[512,2048]{1,0:T(8,128)(2,1)S(1)} %copy-done, f32[2048]{0:T(1024)S(1)} %bitcast.191, f32[2048]{0:T(1024)S(1)} %bitcast.187, f32[512]{0:T(512)S(1)} %fusion.104, ...), kind=kOutput, calls=%fused_computation.199 | convolution fusion | flops 8598323200 | bytes 41963520 | tf_op jit(solution)/shard_map/dot_general | solution.py:52
  1110.4 66.2 %all-reduce.4 = (f32[2048]{0:T(1024)S(1)}, f32[2048]{0:T(1024)S(1)}, f32[2048]{0:T(1024)S(1)}, f32[2048]{0:T(1024)S(1)}, f32[3]{0:T(128)S(1)}) all-reduce(f32[2048]{0:T(1024)S(1)} %get-tuple-element.498, f32[2048]{0:T(1024)S(1)} %get-tuple-element.503, ...), channel_id=3, replica_groups=mesh['dp'=4,'ctx'=4,'tp'=2] {'dp','ctx'}, use_global_device_ids=true, to_apply=%region_24.25.clone | all-reduce | flops 8195 | bytes 65560
  1186.1 203.8 %reduce-scatter.17.cloned.1.call-done = f32[128,4096]{0,1:T(8,128)} async-done(((f32[2048,4096]{0,1:T(8,128)}), f32[128,4096]{0,1:T(8,128)}) %reduce-scatter.17.cloned.1.call-update) | async-done | bytes 2097168 | tf_op jit(solution)/shard_map/reduce_scatter | solution.py:179
  1392.8 62.1 %reduce-scatter.11.cloned.1.call-done = f32[128,256]{1,0:T(8,128)} async-done(((f32[2048,256]{1,0:T(8,128)}), f32[128,256]{1,0:T(8,128)}) %reduce-scatter.11.cloned.1.call-update) | async-done | bytes 131088 | tf_op jit(solution)/shard_map/reduce_scatter | solution.py:244
  1454.9 108.7 %reduce-scatter.9.cloned.1.call-done = f32[128,1024]{1,0:T(8,128)} async-done(((f32[2048,1024]{1,0:T(8,128)}), f32[128,1024]{1,0:T(8,128)}) %reduce-scatter.9.cloned.1.call-update) | async-done | bytes 524304 | tf_op jit(solution)/shard_map/reduce_scatter | solution.py:243
  1563.6 109.6 %reduce-scatter.13.cloned.1.call-done = f32[128,1024]{1,0:T(8,128)} async-done(((f32[2048,1024]{1,0:T(8,128)}), f32[128,1024]{1,0:T(8,128)}) %reduce-scatter.13.cloned.1.call-update) | async-done | bytes 524304 | tf_op jit(solution)/shard_map/reduce_scatter | solution.py:245
  1673.2 337.8 %reduce-scatter.15.cloned.1.call-done = f32[128,4096]{1,0:T(8,128)} async-done(((f32[2048,4096]{1,0:T(8,128)}), f32[128,4096]{1,0:T(8,128)}) %reduce-scatter.15.cloned.1.call-update) | async-done | bytes 2097168 | tf_op jit(solution)/shard_map/reduce_scatter | solution.py:178
  (230 shorter events, 393.9 us)
Async XLA Ops:
  7.2 70.6 %all-gather.10.cloned.1.call-start = ((), (), s32[]{:S(2)}) async-start(), calls=%async_computation.6 | async-start | bytes 1114112 | tf_op jit(solution)/shard_map/all_gather | solution.py:72
  7.9 100.2 %all-gather.12.cloned.1.call-start = ((), (), s32[]{:S(2)}) async-start(), calls=%async_computation.7 | async-start | bytes 1310720 | tf_op jit(solution)/shard_map/all_gather | solution.py:85
  81.1 79.5 %all-gather.14.cloned.1.call-start = ((), (), s32[]{:S(2)}) async-start(), calls=%async_computation.8 | async-start | bytes 4456448 | tf_op jit(solution)/shard_map/all_gather | solution.py:71
  81.9 129.9 %all-gather.16.cloned.1.call-start = ((), (), s32[]{:S(2)}) async-start(), calls=%async_computation.9 | async-start | bytes 4456448 | tf_op jit(solution)/shard_map/all_gather | solution.py:73
  82.4 616.2 %all-reduce.11.cloned.1.call-start = ((), (), s32[]{:S(2)}) async-start(), calls=%async_computation.10 | async-start | bytes 4194304 | tf_op jit(solution)/shard_map/psum | solution.py:132
  217.7 484.3 %all-gather.18.cloned.1.call-start = ((), (), s32[]{:S(2)}) async-start(), calls=%async_computation.11 | async-start | bytes 17825792 | tf_op jit(solution)/shard_map/all_gather | solution.py:140
  218.2 660.5 %all-reduce.15.cloned.1.call-start = ((), (), s32[]{:S(2)}) async-start(), calls=%async_computation.19 | async-start | bytes 8388608 | tf_op jit(solution)/shard_map/psum | solution.py:149
  219.8 47.7 %collective-permute-start.1 = (bf16[128,4096]{1,0:T(8,128)(2,1)}, bf16[128,4096]{1,0:T(8,128)(2,1)S(1)}, u32[]{:S(2)}, u32[]{:S(2)}) collective-permute-start(bf16[128,4096]{1,0:T(8,128)(2,1)} %param.25), channel_id=1, source_target_pairs={{0,30},{2,0},{4,2},{6,4},{8,6},{10,8},{12,10},{14,12},{16,14},{18,... | collective-permute-start | bytes 3145736 | tf_op jit(solution)/shard_map/ppermute | solution.py:23
  246.7 45.1 %collective-permute-start.2 = (bf16[128,4096]{1,0:T(8,128)(2,1)S(1)}, bf16[128,4096]{1,0:T(8,128)(2,1)}, u32[]{:S(2)}, u32[]{:S(2)}) collective-permute-start(bf16[128,4096]{1,0:T(8,128)(2,1)S(1)} %collective-permute-done), channel_id=1, source_target_pairs={{0,2},{2,4},{4,6},{6,8},{8,10},{10,12},{12,14},{14,16},{16,18},{18... | collective-permute-start | bytes 3145736 | tf_op jit(solution)/shard_map/ppermute | solution.py:20
  267.5 96.4 %collective-permute-start.3 = (bf16[128,4096]{1,0:T(8,128)(2,1)S(1)}, bf16[128,4096]{1,0:T(8,128)(2,1)}, u32[]{:S(2)}, u32[]{:S(2)}) collective-permute-start(bf16[128,4096]{1,0:T(8,128)(2,1)S(1)} %collective-permute-done.1), channel_id=1, source_target_pairs={{0,30},{2,0},{4,2},{6,4},{8,6},{10,8},{12,10},{14,12},{16,14},{18,... | collective-permute-start | bytes 3145736 | tf_op jit(solution)/shard_map/ppermute | solution.py:23
  291.8 78.6 %collective-permute-start.4 = (bf16[128,4096]{1,0:T(8,128)(2,1)}, bf16[128,4096]{1,0:T(8,128)(2,1)}, u32[]{:S(2)}, u32[]{:S(2)}) collective-permute-start(bf16[128,4096]{1,0:T(8,128)(2,1)} %collective-permute-done.2), channel_id=1, source_target_pairs={{0,2},{2,4},{4,6},{6,8},{8,10},{10,12},{12,14},{14,16},{16,18},{18... | collective-permute-start | bytes 3145736 | tf_op jit(solution)/shard_map/ppermute | solution.py:20
  363.9 151.6 %collective-permute-start.5 = (bf16[128,4096]{1,0:T(8,128)(2,1)}, bf16[128,4096]{1,0:T(8,128)(2,1)S(1)}, u32[]{:S(2)}, u32[]{:S(2)}) collective-permute-start(bf16[128,4096]{1,0:T(8,128)(2,1)} %collective-permute-done.3), channel_id=1, source_target_pairs={{0,30},{2,0},{4,2},{6,4},{8,6},{10,8},{12,10},{14,12},{16,14},{18,... | collective-permute-start | bytes 3145736 | tf_op jit(solution)/shard_map/ppermute | solution.py:23
  370.4 148.4 %collective-permute-start.6 = (bf16[128,4096]{1,0:T(8,128)(2,1)}, bf16[128,4096]{1,0:T(8,128)(2,1)}, u32[]{:S(2)}, u32[]{:S(2)}) collective-permute-start(bf16[128,4096]{1,0:T(8,128)(2,1)} %collective-permute-done.4), channel_id=1, source_target_pairs={{0,2},{2,4},{4,6},{6,8},{8,10},{10,12},{12,14},{14,16},{16,18},{18... | collective-permute-start | bytes 3145736 | tf_op jit(solution)/shard_map/ppermute | solution.py:20
  540.1 46.0 %collective-permute-start.9 = (bf16[128,4096]{1,0:T(8,128)(2,1)S(1)}, bf16[128,4096]{1,0:T(8,128)(2,1)S(1)}, u32[]{:S(2)}, u32[]{:S(2)}) collective-permute-start(bf16[128,4096]{1,0:T(8,128)(2,1)S(1)} %collective-permute-done.7), channel_id=1, source_target_pairs={{0,30},{2,0},{4,2},{6,4},{8,6},{10,8},{12,10},{14,12},{16,14},{18,... | collective-permute-start | bytes 3145736 | tf_op jit(solution)/shard_map/ppermute | solution.py:23
  586.2 45.0 %collective-permute-start.11 = (bf16[128,4096]{1,0:T(8,128)(2,1)S(1)}, bf16[128,4096]{1,0:T(8,128)(2,1)S(1)}, u32[]{:S(2)}, u32[]{:S(2)}) collective-permute-start(bf16[128,4096]{1,0:T(8,128)(2,1)S(1)} %collective-permute-done.9), channel_id=1, source_target_pairs={{0,30},{2,0},{4,2},{6,4},{8,6},{10,8},{12,10},{14,12},{16,14},{18,... | collective-permute-start | bytes 3145736 | tf_op jit(solution)/shard_map/ppermute | solution.py:23
  607.6 45.0 %collective-permute-start.12 = (bf16[128,4096]{1,0:T(8,128)(2,1)S(1)}, bf16[128,4096]{1,0:T(8,128)(2,1)S(1)}, u32[]{:S(2)}, u32[]{:S(2)}) collective-permute-start(bf16[128,4096]{1,0:T(8,128)(2,1)S(1)} %collective-permute-done.10), channel_id=1, source_target_pairs={{0,2},{2,4},{4,6},{6,8},{8,10},{10,12},{12,14},{14,16},{16,18},{18... | collective-permute-start | bytes 3145736 | tf_op jit(solution)/shard_map/ppermute | solution.py:20
  631.2 45.0 %collective-permute-start.13 = (bf16[128,4096]{1,0:T(8,128)(2,1)S(1)}, bf16[128,4096]{1,0:T(8,128)(2,1)S(1)}, u32[]{:S(2)}, u32[]{:S(2)}) collective-permute-start(bf16[128,4096]{1,0:T(8,128)(2,1)S(1)} %collective-permute-done.11), channel_id=1, source_target_pairs={{0,30},{2,0},{4,2},{6,4},{8,6},{10,8},{12,10},{14,12},{16,14},{18,... | collective-permute-start | bytes 3145736 | tf_op jit(solution)/shard_map/ppermute | solution.py:23
  769.5 210.7 %reduce-scatter.7.cloned.1.call-start = ((), (), s32[]{:S(2)}) async-start(), calls=%async_computation.12 | async-start | bytes 1310720 | tf_op jit(solution)/shard_map/reduce_scatter | solution.py:226
  915.5 135.3 %all-reduce.13.cloned.1.call-start = ((), (), s32[]{:S(2)}) async-start(), calls=%async_computation.18 | async-start | bytes 4718592 | tf_op jit(solution)/shard_map/psum | solution.py:231
  980.3 409.7 %reduce-scatter.17.cloned.1.call-start = ((), (), s32[]{:S(2)}) async-start(), calls=%async_computation.17 | async-start | bytes 35651584 | tf_op jit(solution)/shard_map/reduce_scatter | solution.py:179
  1001.7 453.2 %reduce-scatter.11.cloned.1.call-start = ((), (), s32[]{:S(2)}) async-start(), calls=%async_computation.14 | async-start | bytes 2228224 | tf_op jit(solution)/shard_map/reduce_scatter | solution.py:244
  1054.5 509.1 %reduce-scatter.9.cloned.1.call-start = ((), (), s32[]{:S(2)}) async-start(), calls=%async_computation.13 | async-start | bytes 8912896 | tf_op jit(solution)/shard_map/reduce_scatter | solution.py:243
  1062.2 611.0 %reduce-scatter.13.cloned.1.call-start = ((), (), s32[]{:S(2)}) async-start(), calls=%async_computation.15 | async-start | bytes 8912896 | tf_op jit(solution)/shard_map/reduce_scatter | solution.py:245
  1072.6 938.4 %reduce-scatter.15.cloned.1.call-start = ((), (), s32[]{:S(2)}) async-start(), calls=%async_computation.16 | async-start | bytes 35651584 | tf_op jit(solution)/shard_map/reduce_scatter | solution.py:178
  (45 other events, 1006.1 us)
Sparse Core Ops, SparseCore 0:
  10.2 40.6 all-gather.9
  81.2 26.8 all-gather.11
  110.3 50.1 all-gather.13
  162.7 49.0 all-gather.15
  217.8 62.2 all-reduce.10
  282.4 202.0 all-gather.17
  769.6 109.0 all-reduce.14
  915.6 64.5 reduce-scatter.6
  983.3 67.4 all-reduce.12
  1054.9 334.9 reduce-scatter.16
  1394.2 60.6 reduce-scatter.10
  1460.0 103.6 reduce-scatter.8
  1568.8 104.3 reduce-scatter.12
  1678.5 332.4 reduce-scatter.14
